TPU v7x, 32 devices: a whole 2x2x4 slice. The times are simulated.
32 devices in a mesh: groups: 2 (over y), ctx: 4 (over z), tm: 2 (over x), tp: 2 (over core).
Axes of the slice: x: 2, y: 2, z: 4, core: 2. Of those that a mesh axis runs over, the one named last changes fastest.
Arguments:
- tokens: bfloat16 [256, 8, 1024], P(('groups', 'tm'), 'ctx'), parts along dimension 0, may hold values from -6 to 6
- norm_gain: float32 [1024], replicated, may hold values from 0.1 to 1.9
- block_mask: int32 [4, 4, 4], P(('groups', 'tm'), 'ctx'), parts along dimension 0, may hold values from 0 to 1, as said below
- w_query: bfloat16 [1024, 1024], P('tm', 'tp'), may hold values from -1.25 to 1.25
- w_key: bfloat16 [1024, 1024], P('tm', 'tp'), may hold values from -1.25 to 1.25
- w_value: bfloat16 [1024, 1024], P('tm', 'tp'), may hold values from -0.1875 to 0.1875
- w_out: bfloat16 [1024, 1024], P('tp', 'tm'), may hold values from -0.1875 to 0.1875
- w_up: bfloat16 [1024, 2048], P('tm', 'tp'), may hold values from -0.1875 to 0.1875
- w_down: bfloat16 [2048, 1024], P('tp', 'tm'), may hold values from -0.125 to 0.125
- conv_weight: float32 [5, 1024], P(None, 'tp'), may hold values from -2.5 to 2.5
Outputs:
- denoised: bfloat16 [256, 8, 1024], P(('groups', 'tm'), 'ctx', 'tp'), parts along dimension 0
There are 2 independent parts, one for each index of `groups`. A program takes and returns all parts, laid end to end along the dimension named above; an argument that names none is the same for every part. Nothing has to cross between parts.
Inputs may be any that keep to these rules, and one draw needn't show every extreme that they name: block_mask[w, i, i] is 1 for every window w and block i.
All inputs are finite; a program needn't handle non-finite values.
Results may differ from a plain program's by a relative error of at most 0.0076.
Values may be sent and summed in bfloat16 or wider, within the bound.
A program may use at most 64 MiB of HBM per device.

v0:
```python
import functools

import jax
import jax.numpy as jnp
from jax import lax
from jax.experimental import pallas as pl
from jax.experimental.pallas import tpu as pltpu
from jax.sharding import PartitionSpec as P

HEAD_DIM = 64
KERNEL = 5


def from_behind(value, axis, steps):
    count = lax.axis_size(axis)
    first, last = (max(0, -steps), min(count, count - steps))
    return lax.ppermute(value, axis, [(source, source + steps) for source in range(first, last)])


def rms_norm(tokens, norm_gain):
    values = tokens.astype(jnp.float32)
    square = jnp.mean(values * values, axis=-1, keepdims=True)
    return (values * lax.rsqrt(square + 1e-05) * norm_gain).astype(jnp.bfloat16)


def on_device(
    tokens, norm_gain, block_mask, w_query, w_key, w_value, w_out, w_up, w_down, conv_weight
):
    frames_here, dancers_here, width = tokens.shape
    rows_here = frames_here * dancers_here
    normed_grid = rms_norm(tokens, norm_gain)
    normed = normed_grid.reshape(rows_here, width)
    pieces = (
        lax.all_gather(w_query, "tm", axis=0, tiled=True),
        lax.all_gather(w_key, "tm", axis=0, tiled=True),
        lax.all_gather(w_value, "tm", axis=0, tiled=True),
        lax.all_gather(w_up, "tm", axis=0, tiled=True),
    )
    query_sum, key_sum, value_sum, hidden = tuple(
        (jnp.dot(normed, piece_one, preferred_element_type=jnp.float32) for piece_one in pieces)
    )
    local_heads = query_sum.shape[1] // HEAD_DIM
    queries = query_sum.astype(jnp.bfloat16).reshape(rows_here, local_heads, HEAD_DIM)
    key_grid = key_sum.astype(jnp.bfloat16).reshape(
        frames_here, dancers_here, local_heads * HEAD_DIM
    )
    value_grid = value_sum.astype(jnp.bfloat16).reshape(
        frames_here, dancers_here, local_heads * HEAD_DIM
    )
    mask_row = block_mask[0, 0].astype(jnp.float32)
    cycle_blocks = mask_row.shape[0]
    key_piece = lax.all_gather(key_grid, "ctx", axis=1, tiled=True)
    value_piece = lax.all_gather(value_grid, "ctx", axis=1, tiled=True)
    count = key_piece.shape[1]
    block_ids = jnp.arange(count) // dancers_here
    picker = (block_ids[:, None] == jnp.arange(cycle_blocks)[None, :]).astype(jnp.float32)
    allowed_dancers = jnp.dot(picker, mask_row)
    peak_old = jnp.full((local_heads, rows_here), -1e30, jnp.float32)
    key_rows = key_piece.reshape(frames_here * count, local_heads, HEAD_DIM)
    value_rows = value_piece.reshape(frames_here * count, local_heads, HEAD_DIM)
    allowed = jnp.tile(allowed_dancers, frames_here)
    scores = (
        jnp.einsum("qhd,khd->hqk", queries, key_rows, preferred_element_type=jnp.float32) * 0.125
    )
    scores = jnp.where(allowed[None, None, :] > 0, scores, -1e30)
    peak_new = jnp.maximum(peak_old, jnp.max(scores, axis=-1))
    expo = jnp.exp(scores - peak_new[:, :, None]) * allowed[None, None, :]
    total_new = jnp.sum(expo, axis=-1)
    probs = expo.astype(jnp.bfloat16)
    mixed_new = jnp.einsum("hqk,khd->hqd", probs, value_rows, preferred_element_type=jnp.float32)
    attended = (
        (mixed_new / total_new[:, :, None])
        .transpose(1, 0, 2)
        .reshape(rows_here, local_heads * HEAD_DIM)
        .astype(jnp.bfloat16)
    )
    activated = jax.nn.gelu(hidden, approximate=True).astype(jnp.bfloat16)
    out_full, down_full = (
        lax.all_gather(w_out, "tm", axis=1, tiled=True),
        lax.all_gather(w_down, "tm", axis=1, tiled=True),
    )
    branches = jnp.dot(attended, out_full, preferred_element_type=jnp.float32)
    branches = branches + jnp.dot(activated, down_full, preferred_element_type=jnp.float32)
    mine = lax.psum_scatter(
        branches.astype(jnp.bfloat16), "tp", scatter_dimension=1, tiled=True
    ).astype(jnp.float32)
    features_here = mine.shape[1]
    first_feature = lax.axis_index("tp") * features_here
    normed_cols = lax.dynamic_slice_in_dim(normed_grid, first_feature, features_here, 2)
    padded = jnp.pad(normed_cols.astype(jnp.float32), ((4, 4), (0, 0), (0, 0)))
    extended = jnp.zeros((frames_here + 4, dancers_here, features_here), jnp.float32)
    for offset in range(KERNEL):
        extended = extended + conv_weight[offset] * padded[offset : offset + frames_here + 4]
    convolved = extended[2 : frames_here + 2]
    from_before = from_behind(extended[frames_here + 2 :], "tm", 1)
    from_after = from_behind(extended[0:2], "tm", -1)
    convolved = convolved.at[0:2].add(from_before)
    convolved = convolved.at[frames_here - 2 :].add(from_after)
    token_cols = lax.dynamic_slice_in_dim(tokens, first_feature, features_here, 2).astype(
        jnp.float32
    )
    result = token_cols + mine.reshape(frames_here, dancers_here, features_here) + convolved
    return result.astype(jnp.bfloat16)


MESH = pl.DeviceIdType.MESH
N_LINE = 4


def normalised(values, gain):
    values = values.astype(jnp.float32)
    square = jnp.mean(values * values, axis=-1, keepdims=True)
    return (values * lax.rsqrt(square + 1e-05) * gain).astype(jnp.bfloat16)


def layer_kernel(
    frame,
    mask_hbm,
    tokens_hbm,
    gain_hbm,
    conv_hbm,
    wq_ref,
    wk_ref,
    wv_ref,
    wup_ref,
    wout_ref,
    wdown_ref,
    out_ref,
    mask_ref,
    gain_ref,
    conv_ref,
    tok_raw,
    normed,
    halo,
    halo_normed,
    bias,
    w_in,
    w_back,
    qkv,
    feats,
    mine,
    summed,
    arrived,
    extended,
    local_sem,
    tok_send,
    tok_recv,
    fwd_send,
    fwd_recv,
    bias_send,
    bias_recv,
    x_send,
    x_recv,
    y_send,
    y_recv,
    back_send,
    back_recv,
    over_send,
    over_recv,
    sib_send,
    sib_recv,
    halo_sem,
    act_send,
    act_recv,
    att_send,
    att_recv,
    red_send,
    red_recv,
):
    g = lax.axis_index("groups")
    c = lax.axis_index("ctx")
    i = lax.axis_index("tm")
    j = lax.axis_index("tp")
    frames, dancers, width = tokens_hbm.shape
    rows = frames * dancers
    half_frames = frames // 2
    depth = wq_ref.shape[0]
    part = depth // 2
    hw = wq_ref.shape[1] // N_LINE
    fw = wup_ref.shape[1] // N_LINE
    cols = out_ref.shape[2]
    heads = hw // HEAD_DIM
    to_x = {"tm": 1 - i}
    to_y = {"groups": 1 - g}
    to_tp = {"tp": 1 - j}

    is_end = lax.rem(lax.div(c + 1, 2), 2) == 0
    e = 1 - lax.rem(lax.div(c + 1, 2), 2)
    is_mid = jnp.logical_not(is_end)
    mate = c + 1 - 2 * lax.rem(c, 2)
    cross = lax.rem(c + 2, N_LINE)
    opp = N_LINE - 1 - c
    first = e * mate + (1 - e) * opp
    second = e * opp + (1 - e) * mate
    slot_first = 2 * (1 - e)
    slot_second = 2 * e
    early = j == i
    late = j != i

    barrier = pltpu.get_barrier_semaphore()
    peers = [to_x, to_y, to_tp, {"ctx": mate}, {"ctx": cross}, {"ctx": opp}, {"tm": 1 - i, "tp": 1 - j}]
    for peer in peers:
        pl.semaphore_signal(barrier, inc=1, device_id=peer, device_id_type=MESH)

    def rows_at(start, size):
        return pl.ds(pl.multiple_of(start, 16), size)

    def cols_at(start, size):
        return pl.ds(pl.multiple_of(start, 128), size)

    own = rows_at(c * rows, rows)
    tok_copy = pltpu.make_async_copy(tokens_hbm, tok_raw.at[c], local_sem.at[6])
    mask_copy = pltpu.make_async_copy(mask_hbm, mask_ref, local_sem.at[9])
    gain_copy = pltpu.make_async_copy(gain_hbm, gain_ref, local_sem.at[7])
    conv_copy = pltpu.make_async_copy(conv_hbm, conv_ref, local_sem.at[8])
    own_depth = rows_at(i * depth, depth)
    in_copies = [
        pltpu.make_async_copy(
            ref.at[:, cols_at(c * hw, hw)],
            w_in.at[own_depth, k * hw : (k + 1) * hw],
            local_sem.at[k],
        )
        for k, ref in enumerate((wq_ref, wk_ref, wv_ref))
    ]
    in_copies.append(
        pltpu.make_async_copy(
            wup_ref.at[:, cols_at(c * fw, fw)],
            w_in.at[own_depth, 3 * hw : 3 * hw + fw],
            local_sem.at[3],
        )
    )
    out_src = wout_ref.at[rows_at(c * hw, hw), :]
    down_src = wdown_ref.at[rows_at(c * fw, fw), :]
    out_rows = rows_at(j * hw, hw)
    down_rows = rows_at(2 * hw + j * fw, fw)
    back_copies = [
        pltpu.make_async_copy(out_src, w_back.at[out_rows], local_sem.at[4]),
        pltpu.make_async_copy(down_src, w_back.at[down_rows], local_sem.at[5]),
    ]
    mask_copy.start()
    tok_copy.start()
    gain_copy.start()
    for copy in in_copies:
        copy.start()
    conv_copy.start()

    @pl.when(early)
    def _():
        for copy in back_copies:
            copy.start()

    sends = []

    def remote(source, target, send, recv, peer):
        return pltpu.make_async_remote_copy(
            src_ref=source,
            dst_ref=target,
            send_sem=send,
            recv_sem=recv,
            device_id=peer,
            device_id_type=MESH,
        )

    def launch(copies, condition=None):
        if condition is None:
            for copy in copies:
                copy.start()
        else:

            @pl.when(condition)
            def _():
                for copy in copies:
                    copy.start()

        sends.append((condition, copies))

    def token_half(block, half):
        return tok_raw.at[block, pl.ds(half * half_frames, half_frames)]

    own_half = tokens_hbm.at[pl.ds(j * half_frames, half_frames)]

    def token_copy(slot, peer, send):
        return remote(own_half, token_half(c, j), tok_send.at[send], tok_recv.at[slot], peer)

    def token_wait(block, slot):
        half = token_half(block, j)
        remote(half, half, tok_send.at[0], tok_recv.at[slot], to_tp).wait_recv()

    pl.semaphore_wait(barrier, len(peers))
    launch(
        [
            token_copy(2, {"ctx": opp}, 0),
            token_copy(0, {"ctx": mate}, 1),
            token_copy(1, {"ctx": cross}, 2),
        ],
        is_end,
    )
    launch([token_copy(2, {"ctx": opp}, 0), token_copy(0, {"ctx": mate}, 1)], is_mid)

    def in_slices(half, owner):
        base = owner * depth + half * part
        out = []
        for k in range(3):
            out.append(w_in.at[rows_at(base, part), k * hw : (k + 1) * hw])
        for k in range(2):
            out.append(w_in.at[rows_at(base + k * (part // 2), part // 2), 3 * hw : 3 * hw + fw])
        return out

    in_sources = [
        ref.at[rows_at(g * part, part), cols_at(c * hw, hw)] for ref in (wq_ref, wk_ref, wv_ref)
    ]
    for k in range(2):
        in_sources.append(
            wup_ref.at[rows_at(g * part + k * (part // 2), part // 2), cols_at(c * fw, fw)]
        )
    x_out = [
        remote(source, ref, x_send.at[k], x_recv.at[k], to_x)
        for k, (source, ref) in enumerate(zip(in_sources, in_slices(g, i)))
    ]
    x_in = [
        remote(ref, ref, x_send.at[k], x_recv.at[k], to_x)
        for k, ref in enumerate(in_slices(g, 1 - i))
    ]
    y_out = [
        remote(ref, ref, y_send.at[k], y_recv.at[k], to_y)
        for k, ref in enumerate(in_slices(g, 1 - i))
    ]
    y_in = [
        remote(ref, ref, y_send.at[k], y_recv.at[k], to_y)
        for k, ref in enumerate(in_slices(1 - g, 1 - i))
    ]
    launch(x_out)

    half_out = hw // 2
    over_peer = {"tm": 1 - i, "tp": i}

    def out_half(core, half):
        return w_back.at[rows_at(core * hw + half * half_out, half_out)]

    def down_whole(core):
        return w_back.at[rows_at(2 * hw + core * fw, fw)]

    launch(
        [
            remote(
                wout_ref.at[rows_at(c * hw + g * half_out, half_out), :],
                out_half(j, g),
                back_send.at[0],
                back_recv.at[j],
                over_peer,
            ),
            remote(down_src, down_whole(j), back_send.at[1], back_recv.at[2 + j], over_peer),
        ]
    )
    back_in = [
        remote(out_half(core, g), out_half(core, g), back_send.at[0], back_recv.at[core], over_peer)
        for core in range(2)
    ]
    down_in = [
        remote(down_whole(core), down_whole(core), back_send.at[1], back_recv.at[2 + core], over_peer)
        for core in range(2)
    ]
    over_out = [
        remote(out_half(core, g), out_half(core, g), over_send.at[core], over_recv.at[core], to_y)
        for core in range(2)
    ]
    over_in = [
        remote(
            out_half(core, 1 - g), out_half(core, 1 - g), over_send.at[core], over_recv.at[core], to_y
        )
        for core in range(2)
    ]
    sib_out = [
        remote(out_src, w_back.at[out_rows], sib_send.at[0], sib_recv.at[0], to_tp),
        remote(down_src, w_back.at[down_rows], sib_send.at[1], sib_recv.at[1], to_tp),
    ]
    launch(sib_out, late)
    their_out = w_back.at[rows_at((1 - j) * hw, hw)]
    their_down = w_back.at[rows_at(2 * hw + (1 - j) * fw, fw)]
    sib_in = [
        remote(their_out, their_out, sib_send.at[0], sib_recv.at[0], to_tp),
        remote(their_down, their_down, sib_send.at[1], sib_recv.at[1], to_tp),
    ]
    halo_copy = remote(
        tokens_hbm.at[pl.ds((1 - i) * (frames - 8), 8)],
        halo,
        halo_sem.at[0],
        halo_sem.at[1],
        to_x,
    )
    launch([halo_copy])
    mask_copy.wait()
    row_ids = lax.broadcasted_iota(jnp.int32, (8, 128), 0)
    tile = jnp.zeros((8, 128), jnp.float32)
    for block in range(N_LINE):
        term = (mask_ref[0, block].astype(jnp.float32) - 1.0) * 1e30
        tile = jnp.where(row_ids == block, term, tile)
    bias[c] = tile

    bias_out, bias_in = [], []
    for slot, peer in enumerate((mate, cross, opp)):
        bias_out.append(
            remote(bias.at[c], bias.at[c], bias_send.at[slot], bias_recv.at[slot], {"ctx": peer})
        )
        bias_in.append(
            remote(
                bias.at[peer], bias.at[peer], bias_send.at[slot], bias_recv.at[slot], {"ctx": peer}
            )
        )
    launch(bias_out)

    gain_copy.wait()
    gain = gain_ref[...]

    def norm_block(block):
        at = rows_at(block * rows, rows)
        normed[at, :] = normalised(tok_raw[block].reshape(rows, width), gain)

    def pass_on(index):
        x_in[index].wait_recv()
        launch([y_out[index]])

    def share(block, slot):
        token_wait(block, slot)
        launch(
            [remote(token_half(block, j), token_half(block, j), fwd_send.at[slot], fwd_recv.at[slot], to_tp)]
        )

    def settle(block, slot):
        half = token_half(block, 1 - j)
        remote(half, half, fwd_send.at[slot], fwd_recv.at[slot], to_tp).wait_recv()
        norm_block(block)

    def project(block):
        at = rows_at(block * rows, rows)
        qkv[at, :] = jnp.dot(
            normed[at, :], w_in[:, 0 : 3 * hw], preferred_element_type=jnp.float32
        ).astype(jnp.bfloat16)

    order = [second, cross, first, c]
    att_cols = cols_at(j * hw, hw)
    act_cols = cols_at(2 * hw + j * fw, fw)

    def feature_copy(index, columns, send, recv):
        ref = feats.at[rows_at(order[index] * rows, rows), columns]
        return remote(ref, ref, send.at[index], recv.at[index], to_tp)

    def feed(index):
        at = rows_at(order[index] * rows, rows)
        hidden = jnp.dot(
            normed[at, :], w_in[:, 3 * hw : 3 * hw + fw], preferred_element_type=jnp.float32
        )
        feats[at, act_cols] = jax.nn.gelu(hidden, approximate=True).astype(jnp.bfloat16)
        launch([feature_copy(index, act_cols, act_send, act_recv)])

    def attend(index):
        block = order[index]
        at = rows_at(block * rows, rows)
        marks = bias[block]
        mark = jnp.concatenate([marks[k : k + 1, :] for k in range(N_LINE)], axis=1)
        outs = []
        for head in range(heads):
            low = head * HEAD_DIM
            query = qkv[at, low : low + HEAD_DIM]
            key = qkv[:, hw + low : hw + low + HEAD_DIM]
            value = qkv[:, 2 * hw + low : 2 * hw + low + HEAD_DIM]
            scores = lax.dot_general(
                query, key, (((1,), (1,)), ((), ())), preferred_element_type=jnp.float32
            )
            scores = scores * 0.125 + mark
            peak = jnp.max(scores, axis=-1, keepdims=True)
            expo = jnp.exp(scores - peak)
            total = jnp.sum(expo, axis=-1, keepdims=True)
            mixed = jnp.dot(
                expo.astype(jnp.bfloat16), value, preferred_element_type=jnp.float32
            )
            outs.append(mixed / total)
        feats[at, att_cols] = jnp.concatenate(outs, axis=1).astype(jnp.bfloat16)
        launch([feature_copy(index, att_cols, att_send, att_recv)])

    other_att = cols_at((1 - j) * hw, hw)
    other_act = cols_at(2 * hw + (1 - j) * fw, fw)

    def arrive(slot, send, peer):
        copies = []
        for half in range(2):
            at = slice(half * (rows // 2), (half + 1) * (rows // 2))
            copies.append(
                remote(
                    summed.at[send, at],
                    arrived.at[slot, at],
                    red_send.at[2 * send + half],
                    red_recv.at[2 * slot + half],
                    peer,
                )
            )
        return copies

    def wait_arrived(slot, halves=(0, 1)):
        copies = arrive(slot, 0, to_tp)
        for half in halves:
            copies[half].wait_recv()

    end_slots = [0, 1, 2]

    def product(index):
        feature_copy(index, other_att, att_send, att_recv).wait_recv()
        feature_copy(index, other_act, act_send, act_recv).wait_recv()
        at = rows_at(order[index] * rows, rows)
        return jnp.dot(feats[at, :], w_back[...], preferred_element_type=jnp.float32)

    def emit(index):
        value = product(index)
        if index == 3:
            mine[2] = value
            return

        @pl.when(is_end)
        def _():
            summed[index] = value.astype(jnp.bfloat16)
            for copy in arrive(end_slots[index], index, {"ctx": mate}):
                copy.start()

        @pl.when(is_mid)
        def _():
            if index == 0:
                summed[0] = value.astype(jnp.bfloat16)
                for copy in arrive(2, 0, {"ctx": mate}):
                    copy.start()
            else:
                mine[index - 1] = value

    def relay(index):
        peer = {"ctx": cross} if index == 1 else {"ctx": opp}
        copies = arrive(3, index, peer)
        for half in range(2):
            at = slice(half * (rows // 2), (half + 1) * (rows // 2))
            wait_arrived(index - 1, (half,))
            summed[index, at] = (
                mine[index - 1, at] + arrived[index - 1, at].astype(jnp.float32)
            ).astype(jnp.bfloat16)
            copies[half].start()

    def emit_all():
        for index in range(3):
            emit(index)

        @pl.when(is_mid)
        def _():
            relay(1)

        emit(3)

        @pl.when(is_mid)
        def _():
            relay(2)

    tok_copy.wait()
    norm_block(c)
    pass_on(0)
    pass_on(1)
    token_wait(first, slot_first)
    relayed = remote(
        token_half(opp, j), token_half(opp, j), tok_send.at[3], tok_recv.at[1], {"ctx": mate}
    )
    launch([relayed], is_mid)
    launch(
        [
            remote(
                token_half(first, j),
                token_half(first, j),
                fwd_send.at[slot_first],
                fwd_recv.at[slot_first],
                to_tp,
            )
        ]
    )
    pass_on(2)
    settle(first, slot_first)
    pass_on(3)
    share(second, slot_second)
    pass_on(4)
    settle(second, slot_second)
    for copy in y_in[:3]:
        copy.wait_recv()
    for copy in in_copies:
        copy.wait()
    project(c)
    share(cross, 1)
    project(first)
    project(second)
    settle(cross, 1)
    project(cross)

    @pl.when(late)
    def _():
        for core in range(2):
            back_in[core].wait_recv()
            over_out[core].start()

    for copy in bias_in:
        copy.wait_recv()
    attend(0)
    for copy in y_in[3:]:
        copy.wait_recv()
    feed(0)
    attend(1)
    feed(1)

    @pl.when(early)
    def _():
        for copy in back_copies:
            copy.wait()
        for copy in sib_in:
            copy.wait_recv()
        emit(0)

    feed(2)
    feed(3)
    attend(2)

    @pl.when(early)
    def _():
        emit(1)

    attend(3)

    @pl.when(early)
    def _():
        emit(2)

        @pl.when(is_mid)
        def _():
            relay(1)

        emit(3)

        @pl.when(is_mid)
        def _():
            relay(2)

    conv_copy.wait()
    halo_copy.wait_recv()
    halo_normed[...] = normalised(halo[...].reshape(16, width), gain)
    my_cols = cols_at(j * cols, cols)
    edge = halo_normed[:, my_cols].astype(jnp.float32)
    reach = KERNEL // 2
    extended[0:8, :] = jnp.where(i == 1, edge[8:16], 0.0)
    extended[8 : 8 + rows, :] = normed[own, my_cols].astype(jnp.float32)
    extended[8 + rows : 16 + rows, :] = jnp.where(i == 0, edge[0:8], 0.0)
    base = tok_raw[c, :, :, my_cols].reshape(rows, cols).astype(jnp.float32)
    for tap in range(KERNEL):
        shift = 8 + (tap - reach) * frame
        base = base + conv_ref[tap : tap + 1, :] * extended[shift : shift + rows, :]
    mine[3] = base

    @pl.when(late)
    def _():
        for copy in over_in + down_in:
            copy.wait_recv()
        emit_all()

    wait_arrived(2)
    base = mine[3] + mine[2] + arrived[2].astype(jnp.float32)
    wait_arrived(3)
    whole = (base + arrived[3].astype(jnp.float32)).astype(out_ref.dtype)
    out_ref[...] = whole.reshape(frames, dancers, cols)

    @pl.when(late)
    def _():
        for copy in over_out:
            copy.wait_send()

    for index in range(3):
        for copy in arrive(2, index, {"ctx": mate}):
            copy.wait_send()
    for condition, copies in sends:
        if condition is None:
            for copy in copies:
                copy.wait_send()
        else:

            @pl.when(condition)
            def _(copies=copies):
                for copy in copies:
                    copy.wait_send()


def in_one_kernel(
    tokens, norm_gain, block_mask, w_query, w_key, w_value, w_out, w_up, w_down, conv_weight
):
    frames_here, dancers_here, width = tokens.shape
    rows = frames_here * dancers_here
    cols = w_out.shape[1]
    hw = w_query.shape[1] // N_LINE
    fw = w_up.shape[1] // N_LINE
    depth = w_query.shape[0]
    every = N_LINE * rows
    bf16, f32 = jnp.bfloat16, jnp.float32
    vmem = pl.BlockSpec(memory_space=pltpu.VMEM)
    hbm = pl.BlockSpec(memory_space=pltpu.HBM)
    dma = pltpu.SemaphoreType.DMA
    out = pl.pallas_call(
        functools.partial(layer_kernel, dancers_here),
        out_shape=jax.ShapeDtypeStruct((frames_here, dancers_here, cols), bf16),
        in_specs=[hbm] * 10,
        out_specs=vmem,
        scratch_shapes=[
            pltpu.SMEM((1, N_LINE), jnp.int32),
            pltpu.VMEM((1, width), f32),
            pltpu.VMEM(conv_weight.shape, f32),
            pltpu.VMEM((N_LINE,) + tokens.shape, bf16),
            pltpu.VMEM((every, width), bf16),
            pltpu.VMEM((16 // dancers_here, dancers_here, width), bf16),
            pltpu.VMEM((16, width), bf16),
            pltpu.VMEM((N_LINE, 8, 128), f32),
            pltpu.VMEM((2 * depth, 3 * hw + fw), bf16),
            pltpu.VMEM((2 * hw + 2 * fw, cols), bf16),
            pltpu.VMEM((every, 3 * hw), bf16),
            pltpu.VMEM((every, 2 * hw + 2 * fw), bf16),
            pltpu.VMEM((4, rows, cols), f32),
            pltpu.VMEM((3, rows, cols), bf16),
            pltpu.VMEM((4, rows, cols), bf16),
            pltpu.VMEM((rows + 16, cols), f32),
            dma((10,)),
            dma((4,)),
            dma((3,)),
            dma((3,)),
            dma((3,)),
            dma((3,)),
            dma((3,)),
            dma((5,)),
            dma((5,)),
            dma((5,)),
            dma((5,)),
            dma((2,)),
            dma((4,)),
            dma((2,)),
            dma((2,)),
            dma((2,)),
            dma((2,)),
            dma((2,)),
            dma((4,)),
            dma((4,)),
            dma((4,)),
            dma((4,)),
            dma((6,)),
            dma((8,)),
        ],
        compiler_params=pltpu.CompilerParams(
            collective_id=0, has_side_effects=True, vmem_limit_bytes=40 << 20
        ),
    )(
        *[
            pltpu.with_memory_space_constraint(operand, pltpu.HBM)
            for operand in (
                block_mask[0],
                tokens,
                norm_gain[None],
                conv_weight,
                w_query,
                w_key,
                w_value,
                w_up,
                w_out,
                w_down,
            )
        ]
    )
    return out


def solution(mesh):
    def body(tokens, norm_gain, block_mask, w_query, *rest):
        pairs = all(mesh.shape[axis] == 2 for axis in ("groups", "tm", "tp"))
        line = mesh.shape["ctx"] == N_LINE
        rows = tokens.shape[0] * tokens.shape[1]
        split = w_query.shape[1] == 128 * N_LINE and tokens.shape[1] * (KERNEL // 2) <= 8
        if pairs and line and split and rows == 128 and tokens.shape[1] == 2:
            return in_one_kernel(tokens, norm_gain, block_mask, w_query, *rest)
        return on_device(tokens, norm_gain, block_mask, w_query, *rest)

    placed = (
        P(("groups", "tm"), "ctx", None),
        P(),
        P(("groups", "tm"), "ctx", None),
        P("tm", "tp"),
        P("tm", "tp"),
        P("tm", "tp"),
        P("tp", "tm"),
        P("tm", "tp"),
        P("tp", "tm"),
        P(None, "tp"),
    )
    return jax.shard_map(
        body,
        mesh=mesh,
        in_specs=placed,
        out_specs=P(("groups", "tm"), "ctx", "tp"),
        check_vma=False,
    )
```

profile of v0, /device:TPU:14, one launch (start us, length us, event | category | flops | bytes accessed | tf_op | source)
XLA Modules:
  0.0 32.6 jit_solution(14618113487169679347)
XLA Ops:
  0.0 31.9 %shard_map.100 = bf16[64,2,512]{2,1,0:T(2,128)(2,1)S(1)} custom-call(s32[1,4]{1,0:T(1,128)} %bitcast.3, bf16[64,2,1024]{2,1,0:T(2,128)(2,1)} %tokens_hbm.1, f32[1,1024]{1,0:T(1,128)} %bitcast.2, f32[5,512]{1,0:T(8,128)} %conv_hbm.1, bf16[512,512]{1,0:T(8,128)(2,1)} %wq_ref.1, bf16[512,512]{1,0:T(8,128)(2,1)} %wk_ref.1, bf16[512,512]{1,0:T(8,128)(2,1)} %wv_ref.1, ...), custom_call_target="tpu_custom_call" | custom-call | tf_op jit(solution)/shard_map/pallas_call | solution.py:703
  31.9 0.7 %copy.12 = bf16[64,2,512]{2,1,0:T(2,128)(2,1)} copy(bf16[64,2,512]{2,1,0:T(2,128)(2,1)S(1)} %shard_map.100) | data formatting | bytes 262144
where the time goes:
time: 32.7 us; the launch traced here: 32.6 us
  Pallas kernels  31.9 us (98%)
  local copies, waits for them, and re-layouts  0.66 us (2%)
    pallas_call x1, Pallas kernels, in_one_kernel(): pl.pallas_call(functools.partial(layer_kernel, dancers_here), out_shape=j...  31.9 us
    unnamed x1, local copies, waits for them, and re-layouts  0.66 us

commit v1 on v0

--- a/solution.py
+++ b/solution.py
@@ -111,6 +111,9 @@
     values = values.astype(jnp.float32)
     square = jnp.mean(values * values, axis=-1, keepdims=True)
     return (values * lax.rsqrt(square + 1e-05) * gain).astype(jnp.bfloat16)
+
+
+PIECES = 4
 
 
 def layer_kernel(
@@ -289,8 +292,8 @@
     pl.semaphore_wait(barrier, len(peers))
     launch(
         [
+            token_copy(0, {"ctx": mate}, 1),
             token_copy(2, {"ctx": opp}, 0),
-            token_copy(0, {"ctx": mate}, 1),
             token_copy(1, {"ctx": cross}, 2),
         ],
         is_end,
@@ -332,13 +335,18 @@
     launch(x_out)
 
     half_out = hw // 2
+    half_down = fw // 2
+    quarter_down = fw // 4
     over_peer = {"tm": 1 - i, "tp": i}
 
     def out_half(core, half):
         return w_back.at[rows_at(core * hw + half * half_out, half_out)]
 
-    def down_whole(core):
-        return w_back.at[rows_at(2 * hw + core * fw, fw)]
+    def down_late(core):
+        return w_back.at[rows_at(2 * hw + core * fw + half_down, half_down)]
+
+    def down_quarter(core, half):
+        return w_back.at[rows_at(2 * hw + core * fw + half * quarter_down, quarter_down)]
 
     launch(
         [
@@ -349,15 +357,38 @@
                 back_recv.at[j],
                 over_peer,
             ),
-            remote(down_src, down_whole(j), back_send.at[1], back_recv.at[2 + j], over_peer),
+            remote(
+                wdown_ref.at[rows_at(c * fw + g * quarter_down, quarter_down), :],
+                down_quarter(j, g),
+                back_send.at[2],
+                back_recv.at[4 + j],
+                over_peer,
+            ),
+            remote(
+                wdown_ref.at[rows_at(c * fw + half_down, half_down), :],
+                down_late(j),
+                back_send.at[1],
+                back_recv.at[2 + j],
+                over_peer,
+            ),
         ]
     )
     back_in = [
         remote(out_half(core, g), out_half(core, g), back_send.at[0], back_recv.at[core], over_peer)
         for core in range(2)
     ]
+    back_in += [
+        remote(
+            down_quarter(core, g),
+            down_quarter(core, g),
+            back_send.at[2],
+            back_recv.at[4 + core],
+            over_peer,
+        )
+        for core in range(2)
+    ]
     down_in = [
-        remote(down_whole(core), down_whole(core), back_send.at[1], back_recv.at[2 + core], over_peer)
+        remote(down_late(core), down_late(core), back_send.at[1], back_recv.at[2 + core], over_peer)
         for core in range(2)
     ]
     over_out = [
@@ -367,6 +398,26 @@
     over_in = [
         remote(
             out_half(core, 1 - g), out_half(core, 1 - g), over_send.at[core], over_recv.at[core], to_y
+        )
+        for core in range(2)
+    ]
+    over_out += [
+        remote(
+            down_quarter(core, g),
+            down_quarter(core, g),
+            over_send.at[2 + core],
+            over_recv.at[2 + core],
+            to_y,
+        )
+        for core in range(2)
+    ]
+    over_in += [
+        remote(
+            down_quarter(core, 1 - g),
+            down_quarter(core, 1 - g),
+            over_send.at[2 + core],
+            over_recv.at[2 + core],
+            to_y,
         )
         for core in range(2)
     ]
@@ -483,20 +534,20 @@
 
     def arrive(slot, send, peer):
         copies = []
-        for half in range(2):
-            at = slice(half * (rows // 2), (half + 1) * (rows // 2))
+        for half in range(PIECES):
+            at = slice(half * (rows // PIECES), (half + 1) * (rows // PIECES))
             copies.append(
                 remote(
                     summed.at[send, at],
                     arrived.at[slot, at],
-                    red_send.at[2 * send + half],
-                    red_recv.at[2 * slot + half],
+                    red_send.at[PIECES * send + half],
+                    red_recv.at[PIECES * slot + half],
                     peer,
                 )
             )
         return copies
 
-    def wait_arrived(slot, halves=(0, 1)):
+    def wait_arrived(slot, halves):
         copies = arrive(slot, 0, to_tp)
         for half in halves:
             copies[half].wait_recv()
@@ -533,8 +584,8 @@
     def relay(index):
         peer = {"ctx": cross} if index == 1 else {"ctx": opp}
         copies = arrive(3, index, peer)
-        for half in range(2):
-            at = slice(half * (rows // 2), (half + 1) * (rows // 2))
+        for half in range(PIECES):
+            at = slice(half * (rows // PIECES), (half + 1) * (rows // PIECES))
             wait_arrived(index - 1, (half,))
             summed[index, at] = (
                 mine[index - 1, at] + arrived[index - 1, at].astype(jnp.float32)
@@ -542,8 +593,7 @@
             copies[half].start()
 
     def emit_all():
-        for index in range(3):
-            emit(index)
+        emit(2)
 
         @pl.when(is_mid)
         def _():
@@ -581,12 +631,12 @@
     share(second, slot_second)
     pass_on(4)
     settle(second, slot_second)
+    share(cross, 1)
     for copy in y_in[:3]:
         copy.wait_recv()
     for copy in in_copies:
         copy.wait()
     project(c)
-    share(cross, 1)
     project(first)
     project(second)
     settle(cross, 1)
@@ -594,7 +644,7 @@
 
     @pl.when(late)
     def _():
-        for core in range(2):
+        for core in range(4):
             back_in[core].wait_recv()
             over_out[core].start()
 
@@ -623,6 +673,13 @@
     def _():
         emit(1)
 
+    @pl.when(late)
+    def _():
+        for copy in over_in + down_in:
+            copy.wait_recv()
+        emit(0)
+        emit(1)
+
     attend(3)
 
     @pl.when(early)
@@ -638,6 +695,10 @@
         @pl.when(is_mid)
         def _():
             relay(2)
+
+    @pl.when(late)
+    def _():
+        emit_all()
 
     conv_copy.wait()
     halo_copy.wait_recv()
@@ -654,17 +715,17 @@
         base = base + conv_ref[tap : tap + 1, :] * extended[shift : shift + rows, :]
     mine[3] = base
 
-    @pl.when(late)
-    def _():
-        for copy in over_in + down_in:
-            copy.wait_recv()
-        emit_all()
-
-    wait_arrived(2)
-    base = mine[3] + mine[2] + arrived[2].astype(jnp.float32)
-    wait_arrived(3)
-    whole = (base + arrived[3].astype(jnp.float32)).astype(out_ref.dtype)
-    out_ref[...] = whole.reshape(frames, dancers, cols)
+    mine[3] = mine[3] + mine[2]
+    count = PIECES
+    for piece in range(count):
+        size = rows // count
+        at = slice(piece * size, (piece + 1) * size)
+        wait_arrived(2, (piece,))
+        part_sum = mine[3, at] + arrived[2, at].astype(jnp.float32)
+        wait_arrived(3, (piece,))
+        whole = (part_sum + arrived[3, at].astype(jnp.float32)).astype(out_ref.dtype)
+        span = frames // count
+        out_ref[piece * span : (piece + 1) * span] = whole.reshape(span, dancers, cols)
 
     @pl.when(late)
     def _():
@@ -733,10 +794,10 @@
             dma((5,)),
             dma((5,)),
             dma((5,)),
-            dma((2,)),
+            dma((3,)),
+            dma((6,)),
             dma((4,)),
-            dma((2,)),
-            dma((2,)),
+            dma((4,)),
             dma((2,)),
             dma((2,)),
             dma((2,)),
@@ -744,8 +805,8 @@
             dma((4,)),
             dma((4,)),
             dma((4,)),
-            dma((6,)),
-            dma((8,)),
+            dma((3 * PIECES,)),
+            dma((4 * PIECES,)),
         ],
         compiler_params=pltpu.CompilerParams(
             collective_id=0, has_side_effects=True, vmem_limit_bytes=40 << 20

time: 32.7 us -> 32.1 us (0.982)
  Pallas kernels: 31.9 us -> 31.1 us
    pallas_call x1, Pallas kernels: 31.9 us -> 31.1 us  [in_one_kernel(): pl.pallas_call(functools.partial(layer_kernel, dancers_here), out_shape=j...]
where the time goes in v1:
time: 32.1 us; the launch traced here: 31.8 us
  Pallas kernels  31.1 us (97%)
  local copies, waits for them, and re-layouts  0.66 us (2%)
    pallas_call x1, Pallas kernels, in_one_kernel(): pl.pallas_call(functools.partial(layer_kernel, dancers_here), out_shape=j...  31.1 us
    unnamed x1, local copies, waits for them, and re-layouts  0.66 us

profile of v1, /device:TPU:14, one launch (start us, length us, event | category | flops | bytes accessed | tf_op | source)
XLA Modules:
  0.0 31.8 jit_solution(3308553236417045550)
XLA Ops:
  0.0 31.1 %shard_map.100 = bf16[64,2,512]{2,1,0:T(2,128)(2,1)S(1)} custom-call(s32[1,4]{1,0:T(1,128)} %bitcast.3, bf16[64,2,1024]{2,1,0:T(2,128)(2,1)} %tokens_hbm.1, f32[1,1024]{1,0:T(1,128)} %bitcast.2, f32[5,512]{1,0:T(8,128)} %conv_hbm.1, bf16[512,512]{1,0:T(8,128)(2,1)} %wq_ref.1, bf16[512,512]{1,0:T(8,128)(2,1)} %wk_ref.1, bf16[512,512]{1,0:T(8,128)(2,1)} %wv_ref.1, ...), custom_call_target="tpu_custom_call" | custom-call | tf_op jit(solution)/shard_map/pallas_call | solution.py:764
  31.1 0.7 %copy.12 = bf16[64,2,512]{2,1,0:T(2,128)(2,1)} copy(bf16[64,2,512]{2,1,0:T(2,128)(2,1)S(1)} %shard_map.100) | data formatting | bytes 262144
